TPU v7x, 512 devices: a whole 4x8x8 slice. The times are simulated.
512 devices in a mesh: dp: 8 (over x, y_hi), expert: 64 (over y_lo, z, core).
Axes of the slice: x: 4, y: 8 (y_hi: 2, y_lo: 4; y = y_hi * 4 + y_lo), z: 8, core: 2. Of those that a mesh axis runs over, the one named last changes fastest.
Arguments:
- tokens: bfloat16 [65536, 3584], P(('dp', 'expert')), may hold values from -6 to 6
- out_grad: bfloat16 [65536, 3584], P(('dp', 'expert')), may hold values from -1.1953125 to 1.1953125
- gate_weight: bfloat16 [3584, 32768], P('dp', 'expert'), may hold values from -0.09375 to 0.09375
- up_weight: bfloat16 [3584, 32768], P('dp', 'expert'), may hold values from -0.09375 to 0.09375
- route_ids: int32 [65536, 8], P(('dp', 'expert')), may hold values from 0 to 255, all different within a row; in each aligned block of 128 rows (0 to 127, 128 to 255, ...) at most 6 rows name the same one
- route_weights: float32 [65536, 8], P(('dp', 'expert')), may hold values from 0.02 to 0.5
Outputs:
- grad_down: bfloat16 [32768, 3584], P(('expert', 'dp'))
Inputs may be any that keep to these rules, and one draw needn't show every extreme that they name: `route_ids`: each row names 8 different experts. At most 6 of the rows of one device name any one expert, a bound that some block reaches.
All inputs are finite; a program needn't handle non-finite values.
Results may differ from a plain program's by a relative error of at most 0.015.
Values may be sent and summed in bfloat16 or wider, within the bound.
A program may use at most 128 MiB of HBM per device.

v0:
```python
import jax
import jax.numpy as jnp
from jax import lax
from jax.sharding import PartitionSpec as P

N_ROUTED = 256
LOG_SPLIT = 2


def pack_rows(tokens, out_grad, route_ids, route_weights, experts, row_cap):
    expert_ids = jnp.arange(experts, dtype=jnp.int32)
    matches = route_ids[:, :, None] == expert_ids[None, None, :]
    chosen = jnp.any(matches, axis=1)
    scales = jnp.sum(jnp.where(matches, route_weights[:, :, None], 0.0), axis=1)
    order_rank = jnp.cumsum(chosen.astype(jnp.int32), axis=0) - 1
    slot_ids = jnp.arange(row_cap, dtype=jnp.int32)
    pick_table = chosen.T[:, None, :] & (order_rank.T[:, None, :] == slot_ids[None, :, None])
    pick_flat = pick_table.reshape(experts * row_cap, tokens.shape[0])
    pick_values = pick_flat.astype(jnp.bfloat16)
    sent_rows = jnp.dot(pick_values, tokens, preferred_element_type=jnp.float32).astype(
        jnp.bfloat16
    )
    picked_grads = jnp.dot(pick_values, out_grad, preferred_element_type=jnp.float32)
    slot_scales = jnp.sum(jnp.where(pick_table, scales.T[:, None, :], 0.0), axis=2).reshape(
        experts * row_cap, 1
    )
    scaled = (picked_grads * slot_scales).astype(jnp.bfloat16)
    counts = jnp.sum(chosen.astype(jnp.int32), axis=0)
    return (jnp.stack([sent_rows, scaled]), counts)


def per_device(tokens, out_grad, gate_weight, up_weight, route_ids, route_weights):
    split_count = 2**LOG_SPLIT
    experts = lax.axis_size("expert") // split_count
    feature_count = tokens.shape[1]
    row_cap = max(2, tokens.shape[0] * route_ids.shape[1] * 3 // (2 * N_ROUTED))
    paired, counts = pack_rows(tokens, out_grad, route_ids, route_weights, experts, row_cap)
    spread = jnp.broadcast_to(
        paired.reshape(2, experts, 1, row_cap, feature_count),
        (2, experts, split_count, row_cap, feature_count),
    )
    spread = spread.reshape(2, experts * split_count * row_cap, feature_count)
    received = lax.all_to_all(spread, "expert", split_axis=1, concat_axis=1, tiled=True)
    rows_x = received[0]
    rows_dy = received[1]
    columns = rows_x
    gate_pre = jnp.dot(
        columns,
        lax.all_gather(gate_weight, "dp", axis=0, tiled=True),
        preferred_element_type=jnp.float32,
    )
    up_pre = jnp.dot(
        columns,
        lax.all_gather(up_weight, "dp", axis=0, tiled=True),
        preferred_element_type=jnp.float32,
    )
    hidden = (jax.nn.silu(gate_pre) * up_pre).astype(jnp.bfloat16)
    columns = hidden
    return lax.psum_scatter(
        lax.dot_general(
            columns, rows_dy, (((0,), (0,)), ((), ())), preferred_element_type=jnp.float32
        ).astype(jnp.bfloat16),
        "dp",
        scatter_dimension=0,
        tiled=True,
    )


def solution(mesh):
    return jax.shard_map(
        per_device,
        mesh=mesh,
        in_specs=(
            P(("dp", "expert"), None),
            P(("dp", "expert"), None),
            P("dp", "expert"),
            P("dp", "expert"),
            P(("dp", "expert"), None),
            P(("dp", "expert"), None),
        ),
        out_specs=P(("expert", "dp"), None),
        check_vma=False,
    )
```

profile of v0, /device:TPU:8, one launch (start us, length us, event | category | flops | bytes accessed | tf_op | source)
XLA Modules:
  0.0 417.4 jit_solution(7861766384331546865)
XLA Ops:
  6.5 0.0 copy-start
  6.5 0.8 fusion.18
  7.3 0.1 copy.21
  7.4 0.2 reduce_window_sum.11
  7.6 0.1 copy.22
  7.8 0.1 eq.43
  7.8 0.7 select_reduce_fusion.1
  8.6 0.1 select_reduce_fusion
  8.7 0.1 mul.17
  8.8 0.1 compare_and_fusion
  8.8 0.0 copy-done
  8.9 0.3 fusion
  9.2 0.2 stack.10
  9.4 1.5 convolution_convert_fusion.1
  11.0 0.2 stack.9
  11.2 0.4 maximum_bitcast_fusion
  11.6 1.4 copy.23
  13.1 4.0 broadcast_in_dim.43
  17.1 14.5 %all-to-all-start = ((bf16[2,384,3584]{2,0,1:T(2,128)(2,1)}), bf16[2,384,3584]{2,0,1:T(2,128)(2,1)}, u32[]{:S(2)}, u32[]{:S(2)}) async-start(bf16[2,384,3584]{2,0,1:T(2,128)(2,1)} %bitcast.27), calls=%async_computation | async-start | bytes 11010048 | tf_op jit(solution)/shard_map/all_to_all | solution.py:43
  31.6 0.0 all-gather.3.cloned.1.call-start
  31.6 0.7 all-gather.3.cloned.1.call-update
  32.3 0.0 all-gather.5.cloned.1.call-start
  32.4 0.7 all-gather.5.cloned.1.call-update
  33.1 0.0 reduce-scatter.2.cloned.1.call-start
  33.1 192.5 %all-to-all-done = bf16[2,384,3584]{2,0,1:T(2,128)(2,1)} async-done(((bf16[2,384,3584]{2,0,1:T(2,128)(2,1)}), bf16[2,384,3584]{2,0,1:T(2,128)(2,1)}, u32[]{:S(2)}, u32[]{:S(2)}) %all-to-all-start) | async-done | bytes 5505056 | tf_op jit(solution)/shard_map/all_to_all | solution.py:43
  225.7 14.0 %fusion.21 = (bf16[1,384,3584]{2,0,1:T(2,128)(2,1)}, bf16[1,384,3584]{2,0,1:T(2,128)(2,1)}) fusion(bf16[2,384,3584]{2,0,1:T(2,128)(2,1)} %all-to-all-done), kind=kLoop, calls=%fused_computation.25 | loop fusion | bytes 11010048 | tf_op jit(solution)/shard_map/slice | solution.py:44
  239.7 0.0 all-gather.3.cloned.1.call-done
  239.7 5.2 %fusion.5 = f32[384,512]{1,0:T(8,128)S(1)} fusion(bf16[3584,512]{1,0:T(8,128)(2,1)} %all-gather.3.cloned.1.call-done, bf16[1,384,3584]{2,0,1:T(2,128)(2,1)} %get-tuple-element.5), kind=kOutput, calls=%fused_computation.8 | convolution fusion | flops 1409286144 | bytes 7208960 | tf_op jit(solution)/shard_map/dot_general | solution.py:47
  245.0 41.1 %all-gather.5.cloned.1.call-done = bf16[3584,512]{1,0:T(8,128)(2,1)} async-done(((bf16[448,512]{1,0:T(8,128)(2,1)}), bf16[3584,512]{1,0:T(8,128)(2,1)}) %all-gather.5.cloned.1.call-update) | async-done | bytes 3670032 | tf_op jit(solution)/shard_map/all_gather | solution.py:54
  286.1 10.7 %convolution_convert_fusion = bf16[512,3584]{1,0:T(8,128)(2,1)} fusion(bf16[1,384,3584]{2,0,1:T(2,128)(2,1)} %get-tuple-element.6, bf16[3584,512]{1,0:T(8,128)(2,1)} %all-gather.5.cloned.1.call-done, bf16[1,384,3584]{2,0,1:T(2,128)(2,1)} %get-tuple-element.5, f32[384,512]{1,0:T(8,128)S(1)} %fusion.5), kind=kOutput, calls=%fused_computation | convolution fusion | flops 2821586944 | bytes 13631488 | tf_op jit(solution)/shard_map/dot_general | solution.py:60
  296.8 0.0 reduce-scatter.2.cloned.1.call-update
  296.8 114.0 %reduce-scatter.2.cloned.1.call-done = bf16[64,3584]{1,0:T(8,128)(2,1)} async-done(((bf16[512,3584]{1,0:T(8,128)(2,1)}), bf16[64,3584]{1,0:T(8,128)(2,1)}) %reduce-scatter.2.cloned.1.call-update) | async-done | bytes 458768 | tf_op jit(solution)/shard_map/reduce_scatter | solution.py:59
  (7 shorter events, 0.1 us)
Async XLA Ops:
  6.5 2.3 copy-start
  17.1 208.6 %all-to-all-start = ((bf16[2,384,3584]{2,0,1:T(2,128)(2,1)}), bf16[2,384,3584]{2,0,1:T(2,128)(2,1)}, u32[]{:S(2)}, u32[]{:S(2)}) async-start(bf16[2,384,3584]{2,0,1:T(2,128)(2,1)} %bitcast.27), calls=%async_computation | async-start | bytes 11010048 | tf_op jit(solution)/shard_map/all_to_all | solution.py:43
  31.6 208.1 %all-gather.3.cloned.1.call-start = ((), (), s32[]{:S(2)}) async-start(), calls=%async_computation.2 | async-start | bytes 4128768 | tf_op jit(solution)/shard_map/all_gather | solution.py:49
  32.3 253.8 %all-gather.5.cloned.1.call-start = ((), (), s32[]{:S(2)}) async-start(), calls=%async_computation.3 | async-start | bytes 4128768 | tf_op jit(solution)/shard_map/all_gather | solution.py:54
  33.1 377.7 %reduce-scatter.2.cloned.1.call-start = ((), (), s32[]{:S(2)}) async-start(), calls=%async_computation.4 | async-start | bytes 4128768 | tf_op jit(solution)/shard_map/reduce_scatter | solution.py:59
Sparse Core Ops, SparseCore 0:
  35.6 143.5 all-gather.2
  182.4 103.6 all-gather.4
  297.0 113.8 reduce-scatter.1
where the time goes:
time: 418 us; the launch traced here: 417 us
  waiting for transfers between devices  349 us (83%)
  local copies, waits for them, and re-layouts  20.3 us (5%)
  matrix products  17.8 us (4%)
  starting transfers between devices  14.6 us (3%)
  between operations  13.2 us (3%)
    all_to_all x1, waiting for transfers between devices, per_device(): lax.all_to_all(spread, 'expert', split_axis=1, concat_axis=1, tiled=True)  193 us
    reduce_scatter x1, waiting for transfers between devices, per_device(): lax.psum_scatter(lax.dot_general(columns, rows_dy, (((0,), (0,)), ((), ()...  114 us
    all_gather x1, waiting for transfers between devices, per_device(): lax.all_gather(up_weight, 'dp', axis=0, tiled=True)  41.1 us
    all_to_all x1, starting transfers between devices, per_device(): lax.all_to_all(spread, 'expert', split_axis=1, concat_axis=1, tiled=True)  14.5 us
    slice x1, local copies, waits for them, and re-layouts, per_device(): rows_x = received[0]  14 us
    dot_general x1, matrix products, per_device(): lax.dot_general(columns, rows_dy, (((0,), (0,)), ((), ())), preferred_ele...  10.7 us
  transfers between devices with their start and end apart: 4, of which 3 were waited for; matrix products, arithmetic and copies ran while one was open for 5% of the time, Pallas kernels for 0%

commit v1 on v0

v1 whole, which is shorter than its diff:
```python
import jax
import jax.numpy as jnp
from jax import lax
from jax.experimental import pallas as pl
from jax.experimental.pallas import tpu as pltpu
from jax.sharding import PartitionSpec as P

MESH = pl.DeviceIdType.MESH
F32 = jnp.float32
BF16 = jnp.bfloat16

TOK = 128
DW = 3584
SH = 448
COLS = 512
CAP = 6
NK = 4
TILE = 512
SCHEDULE = (
    "O0", "O1", "D0", "D1", "O2", "D2", "O3", "D3", "S0", "S1", "S2", "S3", "Z0", "Z1",
    "D4", "D5", "Z2", "Z3", "D6", "D7", "Z4", "Z5", "Y0", "P0", "Z6", "Z7", "Y1", "X", "C0",
    "P1", "Y2", "A0", "C1", "P2", "B0", "A1", "Y3", "C2", "P3", "B1", "A2", "C3", "B2",
    "A3", "B3", "E0", "E1", "E2", "E3",
)


def kernel(
    ids_ref, rw_ref, tok_hbm, og_hbm, gw_hbm, uw_hbm, out_ref,
    tok, raw, give, take, send_rows, rows, flat, wts, acc, hid_t, part, hop1, hop2, y_out, y_in, fin,
    local_sem, t_recv, y_recv, o_recv, p_recv, fo_recv, fp_recv,
    d_recv, z_recv, c_recv, h1_recv, h2_recv, ry_recv, send_sem,
):
    dp = lax.axis_index("dp")
    ex = lax.axis_index("expert")
    x, yh = dp // 2, lax.rem(dp, 2)
    yl, z, c = ex // 16, lax.rem(ex // 2, 8), lax.rem(ex, 2)
    zp, par = z // 2, lax.rem(z, 2)

    def dev(x_, yh_, yl_, z_, c_):
        return (x_ * 2 + yh_, (yl_ * 8 + z_) * 2 + c_)

    def ring(x_, d):
        return lax.rem(x_ + d + 4, 4)

    sides = (dev(ring(x, 1), yh, yl, z, c), dev(ring(x, -1), yh, yl, z, c))
    y_dev = dev(x, 1 - yh, yl, z, c)
    z_dev = dev(x, yh, yl, z + 1 - 2 * par, c)
    c_dev = dev(x, yh, yl, z, 1 - c)

    def copy(src, dst, sends, recv, to):
        return pltpu.make_async_remote_copy(
            src_ref=src, dst_ref=dst, send_sem=send_sem.at[sends], recv_sem=recv,
            device_id=to, device_id_type=MESH,
        )

    local = [
        pltpu.make_async_copy(tok_hbm, tok.at[0], local_sem.at[0]),
        pltpu.make_async_copy(og_hbm, tok.at[1], local_sem.at[1]),
        pltpu.make_async_copy(gw_hbm, raw.at[0], local_sem.at[2]),
        pltpu.make_async_copy(uw_hbm, raw.at[1], local_sem.at[3]),
    ]
    for one in local:
        one.start()

    barrier = pltpu.get_barrier_semaphore()

    def greet(to):
        pl.semaphore_signal(barrier, inc=1, device_id=to, device_id_type=MESH)

    for to in (*sides, y_dev, z_dev, c_dev):
        greet(to)
    pair = lax.rem(zp + 3 + 2 * par, 4)
    from_z = (z, 2 * pair, 2 * pair + 1, 2 * lax.rem(zp + 2, 4) + 1 - par)
    odd_out = lax.rem(c + yl + zp, 2)
    odd_in = odd_out
    for jj in range(2):
        for zi in range(4):
            to = dev(x, yh, lax.rem(yl + 8 - odd_in - 2 * jj, 4), from_z[zi], c)
            if jj or zi:
                greet(to)
            else:
                pl.when(odd_in == 1)(lambda to=to: greet(to))
    pl.semaphore_wait(barrier, 12 + odd_out)

    row = lax.broadcasted_iota(jnp.int32, (96, TOK), 0)
    row12 = jnp.zeros((96, TOK), jnp.int32)
    for i in range(1, 8):
        row12 = row12 + jnp.where(row >= 12 * i, 1, 0)
    slot = row - 12 * row12
    is_grad = slot >= CAP
    slot = jnp.where(is_grad, slot - CAP, slot)
    earlier = jnp.where(
        lax.broadcasted_iota(jnp.int32, (TOK, TOK), 0)
        < lax.broadcasted_iota(jnp.int32, (TOK, TOK), 1),
        1.0,
        0.0,
    ).astype(BF16)

    def choice(odd):
        to_zp = (zp + odd + 2 * (row12 >> 2)) & 3
        expert = ((yl + (row12 & 3)) & 3) * 4 + to_zp
        named = jnp.zeros((96, TOK), F32)
        scale = jnp.zeros((96, TOK), F32)
        for k in range(8):
            hit = ids_ref[k : k + 1, :] == expert
            named = jnp.where(hit, 1.0, named)
            scale = scale + jnp.where(hit, rw_ref[k : k + 1, :], 0.0)
        rank = jnp.dot(named.astype(BF16), earlier, preferred_element_type=F32)
        pick = jnp.where(rank == slot.astype(F32), named, 0.0)
        slot_scale = jnp.sum(pick * scale, axis=1, keepdims=True)
        saved = jnp.where(is_grad, 0.0, pick).astype(BF16)
        grads = jnp.where(is_grad, pick, 0.0).astype(BF16)

        def rows_of(at):
            got = jnp.dot(saved, tok[0, :, at], preferred_element_type=F32)
            scaled = jnp.dot(grads, tok[1, :, at], preferred_element_type=F32) * slot_scale
            return (got + scaled).astype(BF16)

        return rows_of

    theirs_of, mine_of = choice(1 - odd_out), choice(odd_out)
    local[0].wait()
    local[1].wait()

    @pl.loop(0, DW // TILE)
    def _(n):
        at = pl.ds(pl.multiple_of(n * TILE, TILE), TILE)
        give[0, :, at] = theirs_of(at)

    copy(give.at[0], take, 13, t_recv.at[0], c_dev).start()

    @pl.loop(0, DW // TILE)
    def _(n):
        at = pl.ds(pl.multiple_of(n * TILE, TILE), TILE)
        give[1, :, at] = mine_of(at)

    local[2].wait()
    local[3].wait()

    def block(owner_x, owner_yh, half=None):
        at = (owner_x * 2 + owner_yh) * SH + (0 if half is None else half * (SH // 2))
        size = SH if half is None else SH // 2
        return pl.ds(pl.multiple_of(at, SH // 2), size)

    mine, theirs = block(x, yh), block(x, 1 - yh)
    lane = lax.broadcasted_iota(jnp.int32, (COLS, 128), 1)
    column = lax.broadcasted_iota(jnp.int32, (COLS, 128), 0) - (lane >> 4) * 64 - (lane & 15)
    for k in range(NK):
        order = jnp.where(column == k * 16, 1.0, 0.0).astype(BF16)
        for a in range(2):
            wts[k, mine, a * 128 : (a + 1) * 128] = jnp.dot(
                raw[a], order, preferred_element_type=F32
            ).astype(BF16)
        for s in range(2):
            copy(wts.at[k, mine], wts.at[k, mine], 3, o_recv.at[s, k], sides[s]).start()

    place = lax.broadcasted_iota(jnp.int32, (192, 96), 0)
    source = lax.broadcasted_iota(jnp.int32, (192, 96), 1)
    place24 = jnp.zeros((192, 96), jnp.int32)
    for i in range(1, 8):
        place24 = place24 + jnp.where(place >= 24 * i, 1, 0)
    within = place - 24 * place24
    grad12 = jnp.where(within >= 12, 1, 0)
    within = within - 12 * grad12
    second = jnp.where(within >= CAP, 1, 0)
    wanted = place24 * 12 + grad12 * CAP + within - CAP * second
    own_place = jnp.where((wanted == source) & (second == 0), 1.0, 0.0).astype(BF16)
    other_place = jnp.where((wanted == source) & (second == 1), 1.0, 0.0).astype(BF16)
    copy(give.at[0], take, 13, t_recv.at[0], c_dev).wait_recv()

    @pl.loop(0, DW // TILE)
    def _(n):
        at = pl.ds(pl.multiple_of(n * TILE, TILE), TILE)
        both = jnp.dot(own_place, give[1, :, at], preferred_element_type=F32) + jnp.dot(
            other_place, take[:, at], preferred_element_type=F32
        )
        send_rows[:, :, :, at] = both.astype(BF16).reshape(8, 3, 8, TILE)

    quarter = c * 16 + par * 8
    for dyl in range(4):
        for j in range(2):
            to_yl, to_zp = lax.rem(yl + dyl, 4), lax.rem(zp + odd_out + 2 * j, 4)
            if j == 0:
                zi, to_par = odd_out * (1 + par), (1 - odd_out) * par
            else:
                zi = 3 + odd_out * (par - 2)
                to_par = (1 - odd_out) * (1 - par) + odd_out
            src = send_rows.at[j * 4 + dyl]
            number = (dyl // 2) * 4 + zi
            dst = rows.at[c * 16 + to_par * 8 + number]
            to = dev(x, yh, to_yl, 2 * to_zp + to_par, c)
            remote = copy(src, dst, 0, d_recv.at[number], to)
            if dyl or j:
                remote.start()
            else:
                pl.when(odd_out == 1)(remote.start)

                @pl.when(odd_out == 0)
                def _():
                    pltpu.make_async_copy(src, dst, d_recv.at[0]).start()

    def pass_on(k, of_yh, recv, recv_next, sends):
        for s in range(2):
            of_x = ring(x, (-1, 1)[s])
            whole, half = block(of_x, of_yh), block(of_x, of_yh, s)
            copy(wts.at[k, whole], wts.at[k, whole], 3, recv.at[s, k], sides[s]).wait_recv()
            copy(wts.at[k, half], wts.at[k, half], sends, recv_next.at[s, k], sides[s]).start()

    def event_o(k):
        pass_on(k, yh, o_recv, fo_recv, 5)

    def event_p(k):
        pass_on(k, 1 - yh, p_recv, fp_recv, 5)

    def event_s(k):
        copy(wts.at[k, mine], wts.at[k, mine], 2, y_recv.at[k], y_dev).start()

    def event_y(k):
        copy(wts.at[k, theirs], wts.at[k, theirs], 2, y_recv.at[k], y_dev).wait_recv()
        for s in range(2):
            copy(wts.at[k, theirs], wts.at[k, theirs], 4, p_recv.at[s, k], sides[s]).start()

    def flatten(first, count):
        at = pl.ds(pl.multiple_of(first * 16, 16), count * 16)
        for a in range(2):
            flat[a, at, :] = rows[pl.ds(first, count), a : a + 2].reshape(count * 16, DW)

    def event_d(number):
        at = quarter + number
        copy(rows.at[at], rows.at[at], 0, d_recv.at[number], z_dev).wait_recv()
        copy(rows.at[at], rows.at[at], 6, z_recv.at[number], z_dev).start()
        copy(rows.at[at], rows.at[at], 8, c_recv.at[0], c_dev).start()
        flatten(at, 1)

    def event_z(number):
        at = c * 16 + (1 - par) * 8 + number
        copy(rows.at[at], rows.at[at], 6, z_recv.at[number], z_dev).wait_recv()
        copy(rows.at[at], rows.at[at], 8, c_recv.at[0], c_dev).start()
        flatten(at, 1)

    def event_x():
        at = pl.ds((1 - c) * 16, 16)
        copy(rows.at[at], rows.at[at], 8, c_recv.at[0], c_dev).wait_recv()

        @pl.loop(0, 8)
        def _(n):
            flatten((1 - c) * 16 + n * 2, 2)

    def owned(of_x, of_yh=None):
        at = of_x * 32 + (0 if of_yh is None else of_yh * 16)
        return pl.ds(pl.multiple_of(at, 16), 32 if of_yh is None else 16)

    def event_c(k):
        for s in range(2):
            for of_yh, recv in ((yh, fo_recv), (1 - yh, fp_recv)):
                half = block(ring(x, 2), of_yh, s)
                copy(wts.at[k, half], wts.at[k, half], 5, recv.at[s, k], sides[s]).wait_recv()
        acc[...] = jnp.zeros_like(acc)

        @pl.loop(0, DW // TILE)
        def _(n):
            at = pl.ds(pl.multiple_of(n * TILE, TILE), TILE)
            acc[...] += jnp.dot(flat[0, :, at], wts[k, at, :], preferred_element_type=F32)

        gate, up = acc[:, 0:128], acc[:, 128:256]
        hidden = jnp.transpose(gate / (1.0 + jnp.exp(-gate)) * up)
        hidden = pltpu.roll(hidden, 4, 1)
        lane16 = lax.broadcasted_iota(jnp.int32, hidden.shape, 1) & 15
        hid_t[...] = jnp.where(lane16 >= 4, hidden, 0.0).astype(BF16)

        @pl.loop(0, DW // TILE)
        def _(n):
            at = pl.ds(pl.multiple_of(n * TILE, TILE), TILE)
            part[k, :, at] = jnp.dot(
                hid_t[...], flat[1, :, at], preferred_element_type=F32
            ).astype(BF16)

        for s in range(2):
            copy(
                part.at[k, owned(ring(x, 2), s)], hop1.at[s, k], 10, h1_recv.at[s, k], sides[s]
            ).start()

    def event_a(k):
        for s in range(2):
            copy(hop1.at[s, k], hop1.at[s, k], 10, h1_recv.at[s, k], sides[s]).wait_recv()
            of_x = ring(x, (1, -1)[s])
            at = owned(of_x, s)
            part[k, at, :] = (
                part[k, at, :].astype(F32) + hop1[s, k].astype(F32)
            ).astype(BF16)
            copy(
                part.at[k, owned(of_x)], hop2.at[s, k], 11, h2_recv.at[s, k], sides[s]
            ).start()

    def event_b(k):
        for s in range(2):
            copy(hop2.at[s, k], hop2.at[s, k], 11, h2_recv.at[s, k], sides[s]).wait_recv()

        def total(of_yh):
            at = pl.ds(pl.multiple_of(of_yh * 16, 16), 16)
            return (
                part[k, owned(x, of_yh), :].astype(F32)
                + hop2[0, k, at, :].astype(F32)
                + hop2[1, k, at, :].astype(F32)
            )

        y_out[k] = total(1 - yh).astype(BF16)
        copy(y_out.at[k], y_in.at[k], 12, ry_recv.at[k], y_dev).start()
        fin[k] = total(yh)

    def event_e(k):
        copy(y_out.at[k], y_in.at[k], 12, ry_recv.at[k], y_dev).wait_recv()
        out_ref[k * 16 : (k + 1) * 16, :] = (fin[k] + y_in[k].astype(F32)).astype(BF16)

    events = dict(
        O=event_o, P=event_p, Y=event_y, S=event_s, D=event_d, Z=event_z, C=event_c,
        A=event_a, B=event_b, E=event_e,
    )
    for name in SCHEDULE:
        if name == "X":
            event_x()
        else:
            events[name[0]](int(name[1]))

    def sent(ref, sends, to):
        copy(ref, ref, sends, o_recv.at[0, 0], to).wait_send()

    sent(give.at[0], 13, c_dev)
    sent(rows.at[pl.ds(0, 8)], 6, z_dev)
    sent(rows.at[pl.ds(0, 16)], 8, c_dev)
    pl.when(odd_out == 0)(lambda: sent(rows.at[pl.ds(0, 7)], 0, z_dev))
    pl.when(odd_out == 1)(lambda: sent(rows.at[pl.ds(0, 8)], 0, z_dev))
    sent(wts.at[0, pl.ds(0, 4 * SH)], 2, y_dev)
    for sends in (3, 4, 5):
        sent(wts.at[0], sends, sides[0])
    sent(flat.at[0, pl.ds(0, 128)], 10, sides[0])
    sent(flat.at[0, pl.ds(0, 256)], 11, sides[0])
    sent(flat.at[0, pl.ds(0, 64)], 12, y_dev)


def per_device(tokens, out_grad, gate_weight, up_weight, route_ids, route_weights):
    vmem = pl.BlockSpec(memory_space=pltpu.VMEM)
    anywhere = pl.BlockSpec(memory_space=pl.ANY)
    dma = pltpu.SemaphoreType.DMA
    return pl.pallas_call(
        kernel,
        out_shape=jax.ShapeDtypeStruct((NK * 16, DW), BF16),
        in_specs=[vmem, vmem, anywhere, anywhere, anywhere, anywhere],
        out_specs=vmem,
        scratch_shapes=[
            pltpu.VMEM((2, TOK, DW), BF16),
            pltpu.VMEM((2, SH, COLS), BF16),
            pltpu.VMEM((2, 96, DW), BF16),
            pltpu.VMEM((96, DW), BF16),
            pltpu.VMEM((8, 3, 8, DW), BF16),
            pltpu.VMEM((32, 3, 8, DW), BF16),
            pltpu.VMEM((2, 512, DW), BF16),
            pltpu.VMEM((NK, 8 * SH, 256), BF16),
            pltpu.VMEM((512, 256), F32),
            pltpu.VMEM((128, 512), BF16),
            pltpu.VMEM((NK, 128, DW), BF16),
            pltpu.VMEM((2, NK, 16, DW), BF16),
            pltpu.VMEM((2, NK, 32, DW), BF16),
            pltpu.VMEM((NK, 16, DW), BF16),
            pltpu.VMEM((NK, 16, DW), BF16),
            pltpu.VMEM((NK, 16, DW), F32),
            dma((4,)),
            dma((1,)),
            dma((NK,)),
            dma((2, NK)),
            dma((2, NK)),
            dma((2, NK)),
            dma((2, NK)),
            dma((8,)),
            dma((8,)),
            dma((1,)),
            dma((2, NK)),
            dma((2, NK)),
            dma((NK,)),
            dma((14,)),
        ],
        compiler_params=pltpu.CompilerParams(
            collective_id=0, has_side_effects=True, vmem_limit_bytes=56 << 20
        ),
        name="routed_grad",
    )(route_ids.T, route_weights.T, tokens, out_grad, gate_weight, up_weight)


def solution(mesh):
    return jax.shard_map(
        per_device,
        mesh=mesh,
        in_specs=(
            P(("dp", "expert"), None),
            P(("dp", "expert"), None),
            P("dp", "expert"),
            P("dp", "expert"),
            P(("dp", "expert"), None),
            P(("dp", "expert"), None),
        ),
        out_specs=P(("expert", "dp"), None),
        check_vma=False,
    )
```

time: 418 us -> 176 us (0.42)
  the two profiles are of different devices: /device:TPU:8 before, /device:TPU:10 now
where the time goes in v1:
time: 176 us
  Pallas kernels  174 us (99%)
  local copies, waits for them, and re-layouts  1.82 us (1%)
    pallas_call x1, Pallas kernels, per_device(): pl.pallas_call(kernel, out_shape=jax.ShapeDtypeStruct((NK * 16, DW), BF16...  174 us

profile of v1, /device:TPU:10, one launch (start us, length us, event | category | flops | bytes accessed | tf_op | source)
XLA Modules:
  0.0 175.7 jit_solution(11483883124445925932)
XLA Ops:
  0.0 173.8 %routed_grad.1 = bf16[64,3584]{1,0:T(8,128)(2,1)} custom-call(s32[8,128]{1,0:T(8,128)} %bitcast.2, f32[8,128]{1,0:T(8,128)} %bitcast.3, bf16[128,3584]{1,0:T(8,128)(2,1)} %tok_hbm.1, bf16[128,3584]{1,0:T(8,128)(2,1)} %og_hbm.1, bf16[448,512]{1,0:T(8,128)(2,1)} %gw_hbm.1, bf16[448,512]{1,0:T(8,128)(2,1)} %uw_hbm.1), custom_call_target="tpu_custom_call" | custom-call | tf_op jit(solution)/shard_map/routed_grad/pallas_call | solution.py:345
  173.8 1.8 %copy.8 = bf16[64,3584]{1,0:T(8,128)(2,1)} copy(bf16[64,3584]{1,0:T(8,128)(2,1)} %routed_grad.1) | data formatting | bytes 917504

commit v2 on v1

--- a/solution.py
+++ b/solution.py
@@ -17,10 +17,10 @@
 NK = 4
 TILE = 512
 SCHEDULE = (
-    "O0", "O1", "D0", "D1", "O2", "D2", "O3", "D3", "S0", "S1", "S2", "S3", "Z0", "Z1",
-    "D4", "D5", "Z2", "Z3", "D6", "D7", "Z4", "Z5", "Y0", "P0", "Z6", "Z7", "Y1", "X", "C0",
-    "P1", "Y2", "A0", "C1", "P2", "B0", "A1", "Y3", "C2", "P3", "B1", "A2", "C3", "B2",
-    "A3", "B3", "E0", "E1", "E2", "E3",
+    "S0", "U0", "U1", "R", "O0", "U2", "D0", "D1", "O1", "U3", "D2", "Y0", "S1", "P0", "D3",
+    "Z0", "Z1", "O2", "D4", "D5", "O3", "Z2", "Z3", "D6", "D7", "Y1", "S2", "P1", "Z4",
+    "Z5", "Y2", "S3", "P2", "Z6", "Z7", "Y3", "P3", "X", "C0", "C1", "A0", "C2", "A1", "B0",
+    "C3", "A2", "B1", "A3", "B2", "B3", "E0", "E1", "E2", "E3",
 )
 
 
@@ -80,7 +80,6 @@
                 greet(to)
             else:
                 pl.when(odd_in == 1)(lambda to=to: greet(to))
-    pl.semaphore_wait(barrier, 12 + odd_out)
 
     row = lax.broadcasted_iota(jnp.int32, (96, TOK), 0)
     row12 = jnp.zeros((96, TOK), jnp.int32)
@@ -126,12 +125,6 @@
     def _(n):
         at = pl.ds(pl.multiple_of(n * TILE, TILE), TILE)
         give[0, :, at] = theirs_of(at)
-
-    copy(give.at[0], take, 13, t_recv.at[0], c_dev).start()
-
-    @pl.loop(0, DW // TILE)
-    def _(n):
-        at = pl.ds(pl.multiple_of(n * TILE, TILE), TILE)
         give[1, :, at] = mine_of(at)
 
     local[2].wait()
@@ -151,8 +144,6 @@
             wts[k, mine, a * 128 : (a + 1) * 128] = jnp.dot(
                 raw[a], order, preferred_element_type=F32
             ).astype(BF16)
-        for s in range(2):
-            copy(wts.at[k, mine], wts.at[k, mine], 3, o_recv.at[s, k], sides[s]).start()
 
     place = lax.broadcasted_iota(jnp.int32, (192, 96), 0)
     source = lax.broadcasted_iota(jnp.int32, (192, 96), 1)
@@ -166,38 +157,44 @@
     wanted = place24 * 12 + grad12 * CAP + within - CAP * second
     own_place = jnp.where((wanted == source) & (second == 0), 1.0, 0.0).astype(BF16)
     other_place = jnp.where((wanted == source) & (second == 1), 1.0, 0.0).astype(BF16)
-    copy(give.at[0], take, 13, t_recv.at[0], c_dev).wait_recv()
-
-    @pl.loop(0, DW // TILE)
-    def _(n):
-        at = pl.ds(pl.multiple_of(n * TILE, TILE), TILE)
-        both = jnp.dot(own_place, give[1, :, at], preferred_element_type=F32) + jnp.dot(
-            other_place, take[:, at], preferred_element_type=F32
-        )
-        send_rows[:, :, :, at] = both.astype(BF16).reshape(8, 3, 8, TILE)
 
     quarter = c * 16 + par * 8
-    for dyl in range(4):
-        for j in range(2):
-            to_yl, to_zp = lax.rem(yl + dyl, 4), lax.rem(zp + odd_out + 2 * j, 4)
-            if j == 0:
-                zi, to_par = odd_out * (1 + par), (1 - odd_out) * par
-            else:
-                zi = 3 + odd_out * (par - 2)
-                to_par = (1 - odd_out) * (1 - par) + odd_out
-            src = send_rows.at[j * 4 + dyl]
-            number = (dyl // 2) * 4 + zi
-            dst = rows.at[c * 16 + to_par * 8 + number]
-            to = dev(x, yh, to_yl, 2 * to_zp + to_par, c)
-            remote = copy(src, dst, 0, d_recv.at[number], to)
-            if dyl or j:
-                remote.start()
-            else:
-                pl.when(odd_out == 1)(remote.start)
-
-                @pl.when(odd_out == 0)
-                def _():
-                    pltpu.make_async_copy(src, dst, d_recv.at[0]).start()
+
+    pl.semaphore_wait(barrier, 12 + odd_out)
+    copy(give.at[0], take, 13, t_recv.at[0], c_dev).start()
+
+    def event_r():
+        copy(give.at[0], take, 13, t_recv.at[0], c_dev).wait_recv()
+
+        @pl.loop(0, DW // TILE)
+        def _(n):
+            at = pl.ds(pl.multiple_of(n * TILE, TILE), TILE)
+            both = jnp.dot(own_place, give[1, :, at], preferred_element_type=F32) + jnp.dot(
+                other_place, take[:, at], preferred_element_type=F32
+            )
+            send_rows[:, :, :, at] = both.astype(BF16).reshape(8, 3, 8, TILE)
+
+        for dyl in range(4):
+            for j in range(2):
+                to_yl, to_zp = lax.rem(yl + dyl, 4), lax.rem(zp + odd_out + 2 * j, 4)
+                if j == 0:
+                    zi, to_par = odd_out * (1 + par), (1 - odd_out) * par
+                else:
+                    zi = 3 + odd_out * (par - 2)
+                    to_par = (1 - odd_out) * (1 - par) + odd_out
+                src = send_rows.at[j * 4 + dyl]
+                number = (dyl // 2) * 4 + zi
+                dst = rows.at[c * 16 + to_par * 8 + number]
+                to = dev(x, yh, to_yl, 2 * to_zp + to_par, c)
+                remote = copy(src, dst, 0, d_recv.at[number], to)
+                if dyl or j:
+                    remote.start()
+                else:
+                    pl.when(odd_out == 1)(remote.start)
+
+                    @pl.when(odd_out == 0)
+                    def _():
+                        pltpu.make_async_copy(src, dst, d_recv.at[0]).start()
 
     def pass_on(k, of_yh, recv, recv_next, sends):
         for s in range(2):
@@ -211,6 +208,10 @@
 
     def event_p(k):
         pass_on(k, 1 - yh, p_recv, fp_recv, 5)
+
+    def event_u(k):
+        for s in range(2):
+            copy(wts.at[k, mine], wts.at[k, mine], 3, o_recv.at[s, k], sides[s]).start()
 
     def event_s(k):
         copy(wts.at[k, mine], wts.at[k, mine], 2, y_recv.at[k], y_dev).start()
@@ -313,12 +314,14 @@
         out_ref[k * 16 : (k + 1) * 16, :] = (fin[k] + y_in[k].astype(F32)).astype(BF16)
 
     events = dict(
-        O=event_o, P=event_p, Y=event_y, S=event_s, D=event_d, Z=event_z, C=event_c,
+        O=event_o, P=event_p, Y=event_y, S=event_s, U=event_u, D=event_d, Z=event_z, C=event_c,
         A=event_a, B=event_b, E=event_e,
     )
     for name in SCHEDULE:
         if name == "X":
             event_x()
+        elif name == "R":
+            event_r()
         else:
             events[name[0]](int(name[1]))
 

time: 176 us -> 149 us (0.85)
  the two profiles are of different devices: /device:TPU:10 before, /device:TPU:216 now
where the time goes in v2:
time: 149 us; the launch traced here: 148 us
  Pallas kernels  147 us (99%)
  local copies, waits for them, and re-layouts  1.82 us (1%)
    pallas_call x1, Pallas kernels, per_device(): pl.pallas_call(kernel, out_shape=jax.ShapeDtypeStruct((NK * 16, DW), BF16...  147 us

profile of v2, /device:TPU:216, one launch (start us, length us, event | category | flops | bytes accessed | tf_op | source)
XLA Modules:
  0.0 148.5 jit_solution(4526614607520287177)
XLA Ops:
  0.0 146.7 %routed_grad.1 = bf16[64,3584]{1,0:T(8,128)(2,1)} custom-call(s32[8,128]{1,0:T(8,128)} %bitcast.2, f32[8,128]{1,0:T(8,128)} %bitcast.3, bf16[128,3584]{1,0:T(8,128)(2,1)} %tok_hbm.1, bf16[128,3584]{1,0:T(8,128)(2,1)} %og_hbm.1, bf16[448,512]{1,0:T(8,128)(2,1)} %gw_hbm.1, bf16[448,512]{1,0:T(8,128)(2,1)} %uw_hbm.1), custom_call_target="tpu_custom_call" | custom-call | tf_op jit(solution)/shard_map/routed_grad/pallas_call | solution.py:348
  146.7 1.8 %copy.8 = bf16[64,3584]{1,0:T(8,128)(2,1)} copy(bf16[64,3584]{1,0:T(8,128)(2,1)} %routed_grad.1) | data formatting | bytes 917504

commit v3 on v2

--- a/solution.py
+++ b/solution.py
@@ -19,7 +19,7 @@
 SCHEDULE = (
     "S0", "U0", "U1", "R", "O0", "U2", "D0", "D1", "O1", "U3", "D2", "Y0", "S1", "P0", "D3",
     "Z0", "Z1", "O2", "D4", "D5", "O3", "Z2", "Z3", "D6", "D7", "Y1", "S2", "P1", "Z4",
-    "Z5", "Y2", "S3", "P2", "Z6", "Z7", "Y3", "P3", "X", "C0", "C1", "A0", "C2", "A1", "B0",
+    "Z5", "Y2", "S3", "P2", "Z6", "Z7", "Y3", "X", "C0", "P3", "C1", "A0", "C2", "A1", "B0",
     "C3", "A2", "B1", "A3", "B2", "B3", "E0", "E1", "E2", "E3",
 )
 
@@ -174,8 +174,8 @@
             )
             send_rows[:, :, :, at] = both.astype(BF16).reshape(8, 3, 8, TILE)
 
-        for dyl in range(4):
-            for j in range(2):
+        for j in range(2):
+            for dyl in range(4):
                 to_yl, to_zp = lax.rem(yl + dyl, 4), lax.rem(zp + odd_out + 2 * j, 4)
                 if j == 0:
                     zi, to_par = odd_out * (1 + par), (1 - odd_out) * par
@@ -258,9 +258,9 @@
                 copy(wts.at[k, half], wts.at[k, half], 5, recv.at[s, k], sides[s]).wait_recv()
         acc[...] = jnp.zeros_like(acc)
 
-        @pl.loop(0, DW // TILE)
+        @pl.loop(0, DW // 896)
         def _(n):
-            at = pl.ds(pl.multiple_of(n * TILE, TILE), TILE)
+            at = pl.ds(pl.multiple_of(n * 896, 896), 896)
             acc[...] += jnp.dot(flat[0, :, at], wts[k, at, :], preferred_element_type=F32)
 
         gate, up = acc[:, 0:128], acc[:, 128:256]
@@ -269,9 +269,9 @@
         lane16 = lax.broadcasted_iota(jnp.int32, hidden.shape, 1) & 15
         hid_t[...] = jnp.where(lane16 >= 4, hidden, 0.0).astype(BF16)
 
-        @pl.loop(0, DW // TILE)
+        @pl.loop(0, DW // 896)
         def _(n):
-            at = pl.ds(pl.multiple_of(n * TILE, TILE), TILE)
+            at = pl.ds(pl.multiple_of(n * 896, 896), 896)
             part[k, :, at] = jnp.dot(
                 hid_t[...], flat[1, :, at], preferred_element_type=F32
             ).astype(BF16)

time: 149 us -> 147 us (0.987)
  the two profiles are of different devices: /device:TPU:216 before, /device:TPU:400 now
where the time goes in v3:
time: 147 us
  Pallas kernels  145 us (99%)
  local copies, waits for them, and re-layouts  1.82 us (1%)
    pallas_call x1, Pallas kernels, per_device(): pl.pallas_call(kernel, out_shape=jax.ShapeDtypeStruct((NK * 16, DW), BF16...  145 us

profile of v3, /device:TPU:400, one launch (start us, length us, event | category | flops | bytes accessed | tf_op | source)
XLA Modules:
  0.0 146.6 jit_solution(11386279605933301739)
XLA Ops:
  0.0 144.7 %routed_grad.1 = bf16[64,3584]{1,0:T(8,128)(2,1)} custom-call(s32[8,128]{1,0:T(8,128)} %bitcast.2, f32[8,128]{1,0:T(8,128)} %bitcast.3, bf16[128,3584]{1,0:T(8,128)(2,1)} %tok_hbm.1, bf16[128,3584]{1,0:T(8,128)(2,1)} %og_hbm.1, bf16[448,512]{1,0:T(8,128)(2,1)} %gw_hbm.1, bf16[448,512]{1,0:T(8,128)(2,1)} %uw_hbm.1), custom_call_target="tpu_custom_call" | custom-call | tf_op jit(solution)/shard_map/routed_grad/pallas_call | solution.py:348
  144.7 1.8 %copy.8 = bf16[64,3584]{1,0:T(8,128)(2,1)} copy(bf16[64,3584]{1,0:T(8,128)(2,1)} %routed_grad.1) | data formatting | bytes 917504
